TPU v7x, 32 devices: a whole 2x2x4 slice. The times are simulated.
32 devices in a mesh: fsdp: 8 (over z, x), seq: 4 (over y, core).
Axes of the slice: x: 2, y: 2, z: 4, core: 2. Of those that a mesh axis runs over, the one named last changes fastest.
Arguments:
- tokens: bfloat16 [16384, 768], P(('fsdp', 'seq')), may hold values from -6 to 6
- read_memory: bfloat16 [8, 10, 768], P('fsdp'), may hold values from -6 to 6
- write_memory: bfloat16 [8, 10, 768], P('fsdp'), may hold values from -6 to 6
- lengths: int32 [8], P('fsdp'), may hold values from 1024 to 2048, as said below
- qkv_weight: bfloat16 [768, 2304], P('fsdp'), may hold values from -0.21875 to 0.21875
- qv_bias: bfloat16 [1536], P('fsdp'), may hold values from -1.5 to 1.5
- out_weight: bfloat16 [768, 768], P('fsdp'), may hold values from -6 to 6
- out_bias: bfloat16 [768], P('fsdp'), may hold values from -1.5 to 1.5
- norm1_gain: bfloat16 [768], P('fsdp'), may hold values from 0.5 to 1.5
- norm1_bias: bfloat16 [768], P('fsdp'), may hold values from -1.5 to 1.5
- up_weight: bfloat16 [768, 3072], P('fsdp'), may hold values from -0.21875 to 0.21875
- up_bias: bfloat16 [3072], P('fsdp'), may hold values from -1.5 to 1.5
- down_weight: bfloat16 [3072, 768], P('fsdp'), may hold values from -0.109375 to 0.109375
- down_bias: bfloat16 [768], P('fsdp'), may hold values from -1.5 to 1.5
- norm2_gain: bfloat16 [768], P('fsdp'), may hold values from 0.5 to 1.5
- norm2_bias: bfloat16 [768], P('fsdp'), may hold values from -1.5 to 1.5
- cotangent: bfloat16 [16384, 768], P(('fsdp', 'seq')), may hold values from -6 to 6
Outputs:
- output: bfloat16 [16384, 768], P(('fsdp', 'seq'))
- input_grad: float32 [16384, 768], P(('fsdp', 'seq'))
- read_grad: float32 [8, 10, 768], P('fsdp')
- write_grad: float32 [8, 10, 768], P('fsdp')
- qkv_weight_grad: float32 [768, 2304], P('fsdp')
- qv_bias_grad: float32 [1536], P('fsdp')
- out_weight_grad: float32 [768, 768], P('fsdp')
- out_bias_grad: float32 [768], P('fsdp')
- norm1_gain_grad: float32 [768], P('fsdp')
- norm1_bias_grad: float32 [768], P('fsdp')
- up_weight_grad: float32 [768, 3072], P('fsdp')
- up_bias_grad: float32 [3072], P('fsdp')
- down_weight_grad: float32 [3072, 768], P('fsdp')
- down_bias_grad: float32 [768], P('fsdp')
- norm2_gain_grad: float32 [768], P('fsdp')
- norm2_bias_grad: float32 [768], P('fsdp')
Inputs may be any that keep to these rules, and one draw needn't show every extreme that they name: `lengths`: valid length of each slot in positions, counting its 10 read and 10 write memory tokens; in every draw some slot has length 2048 and some slot 1024.
All inputs are finite; a program needn't handle non-finite values.
Results may differ from a plain program's by a relative error of at most 0.017.
Values may be sent and summed in bfloat16 or wider, within the bound.
A program may use at most 128 MiB of HBM per device.

v0:
```python
from functools import partial
import jax
import jax.numpy as jnp
from jax import lax
from jax.sharding import PartitionSpec as P

HEAD = 64
MEM = 10
norm_epsilon = 1e-06
masked_score = -1e30


def normalize(values, gain_vec, shift_vec):
    centre = values - jnp.mean(values, axis=-1, keepdims=True)
    factor = lax.rsqrt(jnp.mean(centre * centre, axis=-1, keepdims=True) + norm_epsilon)
    return centre * factor * gain_vec + shift_vec


def over_rows(left, right):
    return lax.dot_general(
        left, right, (((0,), (0,)), ((), ())), preferred_element_type=jnp.float32
    )


def by_columns(left, right):
    return lax.dot_general(
        left, right, (((1,), (1,)), ((), ())), preferred_element_type=jnp.float32
    )


def column_sums(values):
    return jnp.sum(values, axis=0, dtype=jnp.float32)


def per_device(
    tokens,
    read_memory,
    write_memory,
    lengths,
    qkv_weight,
    qv_bias,
    out_weight,
    out_bias,
    norm1_gain,
    norm1_bias,
    up_weight,
    up_bias,
    down_weight,
    down_bias,
    norm2_gain,
    norm2_bias,
    cotangent,
):
    seq_count = lax.axis_size("seq")
    local_rows = tokens.shape[0]
    model_width = tokens.shape[1]
    slot_rows = local_rows * seq_count
    head_cols = model_width // seq_count
    head_count = head_cols // HEAD
    block_rows = min(512, slot_rows)
    block_count = slot_rows // block_rows
    factor = HEAD ** (-0.5)
    length = lengths[0]
    places = lax.axis_index("seq") * local_rows + jnp.arange(local_rows, dtype=jnp.int32)
    in_slot = (places < length)[:, None]
    memory_slots = jnp.arange(MEM, dtype=jnp.int32)
    pick_read = places[:, None] == memory_slots[None, :]
    pick_write = places[:, None] == length - MEM + memory_slots[None, :]
    is_memory = jnp.any(pick_read | pick_write, axis=1)[:, None]
    read_float = pick_read.astype(jnp.float32)
    write_float = pick_write.astype(jnp.float32)
    memory_rows = jnp.dot(
        read_float.astype(jnp.bfloat16), read_memory[0], preferred_element_type=jnp.float32
    ) + jnp.dot(
        write_float.astype(jnp.bfloat16), write_memory[0], preferred_element_type=jnp.float32
    )
    layer_in = jnp.where(is_memory, memory_rows.astype(jnp.bfloat16), tokens)
    qkv_full, qv_full, out_full, out_bias_full, gain_one, shift_one = (
        lax.all_gather(qkv_weight, "fsdp", axis=0, tiled=True),
        lax.all_gather(qv_bias, "fsdp", axis=0, tiled=True),
        lax.all_gather(out_weight, "fsdp", axis=0, tiled=True),
        lax.all_gather(out_bias, "fsdp", axis=0, tiled=True),
        lax.all_gather(norm1_gain, "fsdp", axis=0, tiled=True),
        lax.all_gather(norm1_bias, "fsdp", axis=0, tiled=True),
    )
    projected = jnp.dot(layer_in, qkv_full, preferred_element_type=jnp.float32)
    qv_vec = qv_full.astype(jnp.float32)
    query_tok = (projected[:, :model_width] + qv_vec[:model_width]).astype(jnp.bfloat16)
    keys_tok = projected[:, model_width : 2 * model_width].astype(jnp.bfloat16)
    values_tok = (projected[:, 2 * model_width :] + qv_vec[model_width:]).astype(jnp.bfloat16)
    heads_query, heads_key, heads_value = (
        lax.all_to_all(query_tok, "seq", split_axis=1, concat_axis=0, tiled=True),
        lax.all_to_all(keys_tok, "seq", split_axis=1, concat_axis=0, tiled=True),
        lax.all_to_all(values_tok, "seq", split_axis=1, concat_axis=0, tiled=True),
    )
    heads_query = heads_query.reshape(slot_rows, head_count, HEAD)
    heads_key = heads_key.reshape(slot_rows, head_count, HEAD)
    heads_value = heads_value.reshape(slot_rows, head_count, HEAD)
    key_in_slot = jnp.arange(slot_rows, dtype=jnp.int32) < length

    def scores_for(query_block):
        scores = (
            jnp.einsum("qhd,khd->hqk", query_block, heads_key, preferred_element_type=jnp.float32)
            * factor
        )
        return jnp.where(key_in_slot[None, None, :], scores, masked_score)

    def forward_block(block_index):
        query_block = lax.dynamic_slice_in_dim(heads_query, block_index * block_rows, block_rows, 0)
        scores = scores_for(query_block)
        row_max = jnp.max(scores, axis=-1, keepdims=True)
        exponent = jnp.exp(scores - row_max)
        row_sum = jnp.sum(exponent, axis=-1, keepdims=True)
        probs_low = (exponent / row_sum).astype(jnp.bfloat16)
        mixed_block = jnp.einsum(
            "hqk,khd->qhd", probs_low, heads_value, preferred_element_type=jnp.float32
        )
        return (mixed_block.astype(jnp.bfloat16), row_max, row_sum)

    mixed_blocks, row_maxes, row_sums = lax.map(
        forward_block, jnp.arange(block_count, dtype=jnp.int32)
    )
    mixed_heads = mixed_blocks.reshape(slot_rows, head_cols)
    attended = lax.all_to_all(mixed_heads, "seq", split_axis=0, concat_axis=1, tiled=True)
    branch = jnp.dot(attended, out_full, preferred_element_type=jnp.float32) + out_bias_full.astype(
        jnp.float32
    )
    resid_one = layer_in.astype(jnp.float32) + branch
    middle, norm_one_back = jax.vjp(
        normalize, resid_one, gain_one.astype(jnp.float32), shift_one.astype(jnp.float32)
    )
    up_full, up_bias_full, down_full, down_bias_full, gain_two, shift_two = (
        lax.all_gather(up_weight, "fsdp", axis=0, tiled=True),
        lax.all_gather(up_bias, "fsdp", axis=0, tiled=True),
        lax.all_gather(down_weight, "fsdp", axis=0, tiled=True),
        lax.all_gather(down_bias, "fsdp", axis=0, tiled=True),
        lax.all_gather(norm2_gain, "fsdp", axis=0, tiled=True),
        lax.all_gather(norm2_bias, "fsdp", axis=0, tiled=True),
    )
    middle_low = middle.astype(jnp.bfloat16)
    up_pre = jnp.dot(middle_low, up_full, preferred_element_type=jnp.float32) + up_bias_full.astype(
        jnp.float32
    )
    gelu_out, gelu_back = jax.vjp(partial(jax.nn.gelu, approximate=False), up_pre)
    hidden = gelu_out.astype(jnp.bfloat16)
    down_pre = jnp.dot(
        hidden, down_full, preferred_element_type=jnp.float32
    ) + down_bias_full.astype(jnp.float32)
    final, norm_two_back = jax.vjp(
        normalize, middle + down_pre, gain_two.astype(jnp.float32), shift_two.astype(jnp.float32)
    )
    output = jnp.where(in_slot, final, 0.0).astype(jnp.bfloat16)
    grad_final = jnp.where(in_slot, cotangent.astype(jnp.float32), 0.0)
    down_back, up_back = (
        lax.all_gather(down_weight, "fsdp", axis=0, tiled=True),
        lax.all_gather(up_weight, "fsdp", axis=0, tiled=True),
    )
    grad_resid_two, grad_gain_two, grad_shift_two = norm_two_back(grad_final)
    grad_down = grad_resid_two.astype(jnp.bfloat16)
    grad_down_bias = column_sums(grad_down)
    grad_down_weight = over_rows(hidden, grad_down)
    grad_hidden = by_columns(grad_down, down_back)
    (grad_up_pre,) = gelu_back(grad_hidden)
    grad_up = grad_up_pre.astype(jnp.bfloat16)
    grad_up_bias = column_sums(grad_up)
    grad_up_weight = over_rows(middle_low, grad_up)
    grad_middle = grad_resid_two + by_columns(grad_up, up_back)
    grad_resid_one, grad_gain_one, grad_shift_one = norm_one_back(grad_middle)
    out_back, qkv_back = (
        lax.all_gather(out_weight, "fsdp", axis=0, tiled=True),
        lax.all_gather(qkv_weight, "fsdp", axis=0, tiled=True),
    )
    grad_branch = grad_resid_one.astype(jnp.bfloat16)
    grad_out_bias = column_sums(grad_branch)
    grad_out_weight = over_rows(attended, grad_branch)
    grad_attended = by_columns(grad_branch, out_back).astype(jnp.bfloat16)
    grad_heads = lax.all_to_all(grad_attended, "seq", split_axis=1, concat_axis=0, tiled=True)
    grad_heads = grad_heads.reshape(slot_rows, head_count, HEAD)

    def backward_block(carry, block_item):
        key_sum, value_sum = carry
        block_index, row_max, row_sum = block_item
        query_block = lax.dynamic_slice_in_dim(heads_query, block_index * block_rows, block_rows, 0)
        grad_block = lax.dynamic_slice_in_dim(grad_heads, block_index * block_rows, block_rows, 0)
        scores = scores_for(query_block)
        attn_probs = jnp.exp(scores - row_max) / row_sum
        probs_low = attn_probs.astype(jnp.bfloat16)
        grad_probs = jnp.einsum(
            "qhd,khd->hqk", grad_block, heads_value, preferred_element_type=jnp.float32
        )
        row_delta = jnp.sum(grad_probs * attn_probs, axis=-1, keepdims=True)
        grad_scores = (attn_probs * (grad_probs - row_delta)).astype(jnp.bfloat16)
        grad_query = (
            jnp.einsum("hqk,khd->qhd", grad_scores, heads_key, preferred_element_type=jnp.float32)
            * factor
        )
        key_sum = (
            key_sum
            + jnp.einsum(
                "hqk,qhd->khd", grad_scores, query_block, preferred_element_type=jnp.float32
            )
            * factor
        )
        value_sum = value_sum + jnp.einsum(
            "hqk,qhd->khd", probs_low, grad_block, preferred_element_type=jnp.float32
        )
        return ((key_sum, value_sum), grad_query.astype(jnp.bfloat16))

    zero_heads = jnp.zeros((slot_rows, head_count, HEAD), jnp.float32)
    (key_total, value_total), query_blocks = lax.scan(
        backward_block,
        (zero_heads, zero_heads),
        (jnp.arange(block_count, dtype=jnp.int32), row_maxes, row_sums),
    )
    grad_query_heads = query_blocks.reshape(slot_rows, head_cols)
    grad_key_heads = key_total.reshape(slot_rows, head_cols).astype(jnp.bfloat16)
    grad_value_heads = value_total.reshape(slot_rows, head_cols).astype(jnp.bfloat16)
    grad_query_tok, grad_key_tok, grad_value_tok = (
        lax.all_to_all(grad_query_heads, "seq", split_axis=0, concat_axis=1, tiled=True),
        lax.all_to_all(grad_key_heads, "seq", split_axis=0, concat_axis=1, tiled=True),
        lax.all_to_all(grad_value_heads, "seq", split_axis=0, concat_axis=1, tiled=True),
    )
    grad_projected = jnp.concatenate([grad_query_tok, grad_key_tok, grad_value_tok], axis=1)
    grad_qv_bias = jnp.concatenate([column_sums(grad_query_tok), column_sums(grad_value_tok)])
    grad_qkv_weight = over_rows(layer_in, grad_projected)
    grad_layer_in = grad_resid_one + by_columns(grad_projected, qkv_back)
    input_grad = jnp.where(is_memory, 0.0, grad_layer_in)
    grad_read = lax.dot_general(
        read_float,
        grad_layer_in,
        (((0,), (0,)), ((), ())),
        precision=lax.Precision.HIGHEST,
        preferred_element_type=jnp.float32,
    )
    grad_write = lax.dot_general(
        write_float,
        grad_layer_in,
        (((0,), (0,)), ((), ())),
        precision=lax.Precision.HIGHEST,
        preferred_element_type=jnp.float32,
    )
    (
        shard_qkv,
        shard_qv,
        shard_out_w,
        shard_out_b,
        shard_gain_one,
        shard_shift_one,
        shard_up_w,
        shard_up_b,
        shard_down_w,
        shard_down_b,
        shard_gain_two,
        shard_shift_two,
    ) = (
        lax.psum_scatter(grad_qkv_weight, "fsdp", scatter_dimension=0, tiled=True),
        lax.psum_scatter(grad_qv_bias, "fsdp", scatter_dimension=0, tiled=True),
        lax.psum_scatter(grad_out_weight, "fsdp", scatter_dimension=0, tiled=True),
        lax.psum_scatter(grad_out_bias, "fsdp", scatter_dimension=0, tiled=True),
        lax.psum_scatter(grad_gain_one, "fsdp", scatter_dimension=0, tiled=True),
        lax.psum_scatter(grad_shift_one, "fsdp", scatter_dimension=0, tiled=True),
        lax.psum_scatter(grad_up_weight, "fsdp", scatter_dimension=0, tiled=True),
        lax.psum_scatter(grad_up_bias, "fsdp", scatter_dimension=0, tiled=True),
        lax.psum_scatter(grad_down_weight, "fsdp", scatter_dimension=0, tiled=True),
        lax.psum_scatter(grad_down_bias, "fsdp", scatter_dimension=0, tiled=True),
        lax.psum_scatter(grad_gain_two, "fsdp", scatter_dimension=0, tiled=True),
        lax.psum_scatter(grad_shift_two, "fsdp", scatter_dimension=0, tiled=True),
    )
    (
        sum_qkv,
        sum_qv,
        sum_out_w,
        sum_out_b,
        sum_gain_one,
        sum_shift_one,
        sum_up_w,
        sum_up_b,
        sum_down_w,
        sum_down_b,
        sum_gain_two,
        sum_shift_two,
        read_total,
        write_total,
    ) = (
        lax.psum(shard_qkv.astype(jnp.bfloat16), "seq").astype(jnp.float32),
        lax.psum(shard_qv.astype(jnp.bfloat16), "seq").astype(jnp.float32),
        lax.psum(shard_out_w.astype(jnp.bfloat16), "seq").astype(jnp.float32),
        lax.psum(shard_out_b.astype(jnp.bfloat16), "seq").astype(jnp.float32),
        lax.psum(shard_gain_one.astype(jnp.bfloat16), "seq").astype(jnp.float32),
        lax.psum(shard_shift_one.astype(jnp.bfloat16), "seq").astype(jnp.float32),
        lax.psum(shard_up_w.astype(jnp.bfloat16), "seq").astype(jnp.float32),
        lax.psum(shard_up_b.astype(jnp.bfloat16), "seq").astype(jnp.float32),
        lax.psum(shard_down_w.astype(jnp.bfloat16), "seq").astype(jnp.float32),
        lax.psum(shard_down_b.astype(jnp.bfloat16), "seq").astype(jnp.float32),
        lax.psum(shard_gain_two.astype(jnp.bfloat16), "seq").astype(jnp.float32),
        lax.psum(shard_shift_two.astype(jnp.bfloat16), "seq").astype(jnp.float32),
        lax.psum(grad_read.astype(jnp.bfloat16), "seq").astype(jnp.float32),
        lax.psum(grad_write.astype(jnp.bfloat16), "seq").astype(jnp.float32),
    )
    return (
        output,
        input_grad,
        read_total[None],
        write_total[None],
        sum_qkv,
        sum_qv,
        sum_out_w,
        sum_out_b,
        sum_gain_one,
        sum_shift_one,
        sum_up_w,
        sum_up_b,
        sum_down_w,
        sum_down_b,
        sum_gain_two,
        sum_shift_two,
    )


def solution(mesh):
    in_specs = (
        P(("fsdp", "seq"), None),
        P("fsdp", None, None),
        P("fsdp", None, None),
        P("fsdp"),
        P("fsdp", None),
        P("fsdp"),
        P("fsdp", None),
        P("fsdp"),
        P("fsdp"),
        P("fsdp"),
        P("fsdp", None),
        P("fsdp"),
        P("fsdp", None),
        P("fsdp"),
        P("fsdp"),
        P("fsdp"),
        P(("fsdp", "seq"), None),
    )
    out_specs = (
        P(("fsdp", "seq"), None),
        P(("fsdp", "seq"), None),
        P("fsdp", None, None),
        P("fsdp", None, None),
        P("fsdp", None),
        P("fsdp"),
        P("fsdp", None),
        P("fsdp"),
        P("fsdp"),
        P("fsdp"),
        P("fsdp", None),
        P("fsdp"),
        P("fsdp", None),
        P("fsdp"),
        P("fsdp"),
        P("fsdp"),
    )
    return jax.shard_map(
        per_device, mesh=mesh, in_specs=in_specs, out_specs=out_specs, check_vma=False
    )
```

profile of v0, /device:TPU:0, one launch (start us, length us, event | category | flops | bytes accessed | tf_op | source)
XLA Modules:
  0.0 1022.8 jit_solution(4488948586990560364)
XLA Ops:
  18.6 39.7 %all-reduce.16 = (bf16[1536]{0:T(1024)(128)(2,1)S(1)}, bf16[768]{0:T(1024)(128)(2,1)S(1)}, bf16[768]{0:T(1024)(128)(2,1)S(1)}, bf16[768]{0:T(1024)(128)(2,1)S(1)...) all-reduce(bf16[1536]{0:T(1024)(128)(2,1)S(1)} %dynamic-update-slic, ...), channel_id=1, replica_groups=mesh['fsdp'=8,'seq'=4] {'fsdp'}, use_global_device_ids=true, to_apply=%add | all-reduce | flops 6144 | bytes 24576
  60.5 18.2 %all-gather.6.cloned.1.call-done = bf16[768,2304]{1,0:T(8,128)(2,1)} async-done(((bf16[96,2304]{1,0:T(8,128)(2,1)}), bf16[768,2304]{1,0:T(8,128)(2,1)}) %all-gather.6.cloned.1.call-update) | async-done | bytes 3538960 | tf_op jit(solution)/shard_map/all_gather | solution.py:79
  78.8 4.0 fusion.80
  86.4 3.5 all-to-all-start
  91.0 10.5 %all-to-all-done = bf16[512,4,192]{0,2,1:T(8,128)(2,1)S(1)} async-done(((bf16[512,4,192]{0,2,1:T(8,128)(2,1)}), bf16[512,4,192]{0,2,1:T(8,128)(2,1)S(1)}, u32[]{:S(2)}, u32[]{:S(2)}) %all-to-all-start) | async-done | bytes 786464 | tf_op jit(solution)/shard_map/all_to_all | solution.py:92
  101.5 3.5 all-to-all-start.2
  107.7 9.0 all-to-all-done.2
  116.6 3.5 all-to-all-start.1
  125.5 6.2 all-to-all-done.1
  136.3 44.2 %while.30 = (s32[]{:T(128)}, bf16[4,512,3,64]{1,3,2,0:T(8,128)(2,1)}, f32[4,3,512,1]{2,1,3,0:T(4,128)S(1)}, f32[4,3,512,1]{2,1,3,0:T(4,128)S(1)}, s32[4]{0:T(128...) while((s32[]{:T(128)}, ...), condition=%wide.region_4.5_spmd.clone, body=%wide.region_1.4_spmd.clone.sunk | while | flops 843152384 | bytes 39787204 | solution.py:120
  143.0 4.3 fusion.133
  151.3 2.8 fusion.132
  154.1 4.3 fusion.133
  165.1 4.3 fusion.133
  176.2 4.3 fusion.133
  180.5 3.5 all-to-all-start.3
  184.1 26.3 %all-gather = bf16[8,1,384]{2,1,0:T(2,128)(2,1)S(1)} all-gather(bf16[1,1,384]{2,1,0:T(2,128)(2,1)S(1)} %reshape.204), channel_id=1, replica_groups=mesh['fsdp'=8,'seq'=4] {'fsdp'}, dimensions={0}, use_global_device_ids=true | all-gather | bytes 6912 | tf_op jit(solution)/shard_map/all_gather | solution.py:134
  214.5 20.9 %multiply_convert_fusion.1 = (bf16[512,3072]{1,0:T(8,128)(2,1)}, f32[512,3072]{1,0:T(8,128)}, f32[512,3072]{1,0:T(8,128)}) fusion(f32[3072]{0:T(1024)S(1)} %bitcast.154, bf16[768,3072]{1,0:T(8,128)(2,1)} %all-gather.10.cloned.1.call-done, f32[512,768]{1,0:T(8,128)} %copy-done.7, f32[768]{0:T(1024)S(1)} %convert_element_type.216, ...), kind=kOutput, calls=%fused_computation.49 | convolution fusion | flops 2521694208 | bytes 22042624 | tf_op jit(solution)/shard_map/dot_general | solution.py:141
  235.4 46.2 %all-gather.12.cloned.1.call-done = bf16[3072,768]{1,0:T(8,128)(2,1)} async-done(((bf16[384,768]{1,0:T(8,128)(2,1)}), bf16[3072,768]{1,0:T(8,128)(2,1)}) %all-gather.12.cloned.1.call-update) | async-done | bytes 4718608 | tf_op jit(solution)/shard_map/all_gather | solution.py:135
  281.6 6.1 fusion.79
  292.0 8.9 convert_reduce_fusion
  300.9 3.6 multiply_reduce_fusion.2
  309.1 4.2 all-to-all-start.4
  313.4 3.4 fusion.81
  316.8 8.2 all-to-all-done.4
  331.4 115.4 %while.31 = (s32[]{:T(128)}, f32[2048,3,64]{0,2,1:T(8,128)S(1)}, f32[2048,3,64]{0,2,1:T(8,128)}, bf16[4,512,3,64]{1,3,2,0:T(8,128)(2,1)}, s32[4]{0:T(128)S(1)}, ...) while((s32[]{:T(128)}, f32[2048,3,64]{0,2,1:T(8,128)S(1)}, ...), condition=%wide.region_15.16_spmd.clone, body=%wide.region_13.15_spmd.clone.sunk | while | flops 2046886400 | bytes 204722992 | solution.py:210
  333.4 4.3 exponential_divide_fusion.2
  337.7 3.3 multiply_reduce_fusion.8
  342.2 3.5 multiply_convert_fusion.3
  345.7 4.5 fusion.143
  350.2 6.3 fusion.145
  356.5 3.4 fusion.144
  361.8 4.3 exponential_divide_fusion.2
  366.2 3.2 multiply_reduce_fusion.8
  370.7 3.5 multiply_convert_fusion.3
  374.2 4.5 fusion.143
  378.6 6.3 fusion.145
  385.0 4.0 fusion.144
  390.9 4.3 exponential_divide_fusion.2
  395.2 3.2 multiply_reduce_fusion.8
  399.7 3.5 multiply_convert_fusion.3
  403.2 4.4 fusion.143
  407.7 6.3 fusion.145
  413.9 4.0 fusion.144
  419.8 4.3 exponential_divide_fusion.2
  424.2 3.2 multiply_reduce_fusion.8
  428.7 3.5 multiply_convert_fusion.3
  432.2 4.4 fusion.143
  436.6 6.3 fusion.145
  442.9 4.0 fusion.144
  448.6 3.5 all-to-all-start.6
  454.5 9.2 all-to-all-done.6
  463.7 14.1 %all_to_all.134 = bf16[4,512,192]{1,2,0:T(8,128)(2,1)S(1)} all-to-all(bf16[4,512,192]{1,2,0:T(8,128)(2,1)S(1)} %copy.93), channel_id=1, replica_groups=mesh['fsdp'=8,'seq'=4] {'seq'}, dimensions={0} | all-to-all | bytes 1572864 | tf_op jit(solution)/shard_map/all_to_all | solution.py:221
  477.8 14.3 %all_to_all.135 = bf16[4,512,192]{1,2,0:T(8,128)(2,1)S(1)} all-to-all(bf16[4,512,192]{1,2,0:T(8,128)(2,1)S(1)} %bitcast.149), channel_id=1, replica_groups=mesh['fsdp'=8,'seq'=4] {'seq'}, dimensions={0} | all-to-all | bytes 1572864 | tf_op jit(solution)/shard_map/all_to_all | solution.py:219
  492.0 6.4 fusion.51
  499.5 8.2 fusion.82
  509.2 7.2 fusion.69
  519.1 37.6 %all-reduce.15 = (bf16[1536]{0:T(1024)(128)(2,1)S(1)}, bf16[768]{0:T(1024)(128)(2,1)S(1)}, bf16[768]{0:T(1024)(128)(2,1)S(1)}, bf16[768]{0:T(1024)(128)(2,1)S(1)...) all-reduce(f32[1536]{0:T(1024)S(1)} %pad_maximum_fusion.3, ...), channel_id=3, replica_groups=mesh['fsdp'=8,'seq'=4] {'fsdp'}, use_global_device_ids=true, to_apply=%region_22.23.clone | all-reduce | flops 9216 | bytes 55296
  559.2 66.9 %reduce-scatter.5.cloned.1.call-done = f32[96,2304]{1,0:T(8,128)} async-done(((f32[768,2304]{1,0:T(8,128)}), f32[96,2304]{1,0:T(8,128)}) %reduce-scatter.5.cloned.1.call-update) | async-done | bytes 884752 | tf_op jit(solution)/shard_map/reduce_scatter | solution.py:256
  628.1 164.6 %reduce-scatter.11.cloned.1.call-done = f32[384,768]{1,0:T(8,128)} async-done(((f32[3072,768]{1,0:T(8,128)}), f32[384,768]{1,0:T(8,128)}) %reduce-scatter.11.cloned.1.call-update) | async-done | bytes 1179664 | tf_op jit(solution)/shard_map/reduce_scatter | solution.py:264
  794.8 164.3 %reduce-scatter.9.cloned.1.call-done = f32[96,3072]{1,0:T(8,128)} async-done(((f32[768,3072]{1,0:T(8,128)}), f32[96,3072]{1,0:T(8,128)}) %reduce-scatter.9.cloned.1.call-update) | async-done | bytes 1179664 | tf_op jit(solution)/shard_map/reduce_scatter | solution.py:262
  961.4 5.6 broadcast_select_fusion
  968.2 14.3 %all-reduce.17 = (bf16[1,10,768]{2,1,0:T(8,128)(2,1)S(1)}, bf16[1,10,768]{2,1,0:T(8,128)(2,1)S(1)}, bf16[192]{0:T(256)(128)(2,1)S(1)}, bf16[96]{0:T(256)(128)(2,...) all-reduce(bf16[1,10,768]{2,1,0:T(8,128)(2,1)S(1)} %fusion.49, ...), channel_id=1, replica_groups=mesh['fsdp'=8,'seq'=4] {'seq'}, use_global_device_ids=true, to_apply=%region_16.17 | all-reduce | flops 16512 | bytes 66048 | tf_op jit(solution)/shard_map/psum | solution.py:297
  988.0 21.9 %all-reduce.21.cloned.1.call-done = (bf16[96,2304]{1,0:T(8,128)(2,1)}, bf16[96,768]{1,0:T(8,128)(2,1)}, bf16[96,3072]{1,0:T(8,128)(2,1)}, bf16[384,768]{1,0:T(8,128)(2,1)}) async-done(((bf16[96,2304]{1,0:T(8,128)(2,1)}, bf16[96,768]{1,0:T(8,128)(2,1)}, bf16[96,3072]{1,0:T(8,128)(2,1)}, bf16[384,768]{1,0:T(8,128)(2,1)}), (bf16[96,2304]{1,0:T(8,128)(2,1)}, bf16[96,768]{1,0:T(8,128)(2,1)}, ...) | async-done | bytes 1769488 | tf_op jit(solution)/shard_map/psum | solution.py:285
  (276 shorter events, 108.4 us)
Async XLA Ops:
  7.2 51.2 %copy-start = (bf16[1,10,768]{2,1,0:T(8,128)(2,1)S(1)}, bf16[1,10,768]{2,1,0:T(8,128)(2,1)}, u32[]{:S(2)}) copy-start(bf16[1,10,768]{2,1,0:T(8,128)(2,1)} %param.22) | copy-start | bytes 46084
  7.2 71.6 %all-gather.6.cloned.1.call-start = ((), (), s32[]{:S(2)}) async-start(), calls=%async_computation.12 | async-start | bytes 3981312 | tf_op jit(solution)/shard_map/all_gather | solution.py:79
  7.9 202.6 %all-gather.8.cloned.1.call-start = ((), (), s32[]{:S(2)}) async-start(), calls=%async_computation.13 | async-start | bytes 1327104 | tf_op jit(solution)/shard_map/all_gather | solution.py:81
  8.7 205.8 %all-gather.10.cloned.1.call-start = ((), (), s32[]{:S(2)}) async-start(), calls=%async_computation.14 | async-start | bytes 5308416 | tf_op jit(solution)/shard_map/all_gather | solution.py:133
  58.3 24.5 %copy-start.37 = (s32[10]{0:T(128)}, s32[10]{0:T(128)S(1)}, u32[]{:S(2)}) copy-start(s32[10]{0:T(128)S(1)} %iota_add_fusion.1) | copy-start | bytes 124
  58.4 24.4 %copy-start.43 = (pred[512]{0:T(512)(128)(4,1)}, pred[512]{0:T(512)(128)(4,1)S(1)}, u32[]{:S(2)}) copy-start(pred[512]{0:T(512)(128)(4,1)S(1)} %fusion.54) | copy-start | bytes 1540
  60.5 22.3 %copy-start.17 = (bf16[512,768]{1,0:T(8,128)(2,1)}, bf16[512,768]{1,0:T(8,128)(2,1)S(1)}, u32[]{:S(2)}) copy-start(bf16[512,768]{1,0:T(8,128)(2,1)S(1)} %fusion.47) | copy-start | bytes 2359300
  82.8 2.2 copy-start.12
  86.4 15.1 %all-to-all-start = ((bf16[512,4,192]{0,2,1:T(8,128)(2,1)}), bf16[512,4,192]{0,2,1:T(8,128)(2,1)S(1)}, u32[]{:S(2)}, u32[]{:S(2)}) async-start(bf16[512,4,192]{0,2,1:T(8,128)(2,1)} %bitcast.4), calls=%async_computation | async-start | bytes 1572864 | tf_op jit(solution)/shard_map/all_to_all | solution.py:92
  101.5 15.1 %all-to-all-start.2 = ((bf16[512,4,192]{0,2,1:T(8,128)(2,1)}), bf16[512,4,192]{0,2,1:T(8,128)(2,1)S(1)}, u32[]{:S(2)}, u32[]{:S(2)}) async-start(bf16[512,4,192]{0,2,1:T(8,128)(2,1)} %bitcast.8), calls=%async_computation.2 | async-start | bytes 1572864 | tf_op jit(solution)/shard_map/all_to_all | solution.py:94
  116.6 15.1 %all-to-all-start.1 = ((bf16[512,4,192]{0,2,1:T(8,128)(2,1)}), bf16[512,4,192]{0,2,1:T(8,128)(2,1)S(1)}, u32[]{:S(2)}, u32[]{:S(2)}) async-start(bf16[512,4,192]{0,2,1:T(8,128)(2,1)} %bitcast.6), calls=%async_computation.1 | async-start | bytes 1572864 | tf_op jit(solution)/shard_map/all_to_all | solution.py:93
  120.1 161.5 %all-gather.12.cloned.1.call-start = ((), (), s32[]{:S(2)}) async-start(), calls=%async_computation.15 | async-start | bytes 5308416 | tf_op jit(solution)/shard_map/all_gather | solution.py:135
  136.3 47.7 %copy-start.45 = (bf16[384]{0:T(512)(128)(2,1)S(1)}, bf16[384]{0:T(512)(128)(2,1)}, u32[]{:S(2)}) copy-start(bf16[384]{0:T(512)(128)(2,1)} %param.32) | copy-start | bytes 2308
  180.5 34.0 %copy-start.4 = (bf16[2048,3,64]{0,2,1:T(8,128)(2,1)}, bf16[2048,3,64]{0,2,1:T(8,128)(2,1)S(1)}, u32[]{:S(2)}) copy-start(bf16[2048,3,64]{0,2,1:T(8,128)(2,1)S(1)} %get-tuple-element.654) | copy-start | bytes 2359300
  180.5 34.0 %copy-start.6 = (bf16[2048,3,64]{0,2,1:T(8,128)(2,1)}, bf16[2048,3,64]{0,2,1:T(8,128)(2,1)S(1)}, u32[]{:S(2)}) copy-start(bf16[2048,3,64]{0,2,1:T(8,128)(2,1)S(1)} %get-tuple-element.655) | copy-start | bytes 2359300
  180.5 30.0 %all-to-all-start.3 = ((bf16[4,512,192]{1,2,0:T(8,128)(2,1)}), bf16[4,512,192]{1,2,0:T(8,128)(2,1)S(1)}, u32[]{:S(2)}, u32[]{:S(2)}) async-start(bf16[4,512,192]{1,2,0:T(8,128)(2,1)} %bitcast.10), calls=%async_computation.3 | async-start | bytes 1572864 | tf_op jit(solution)/shard_map/all_to_all | solution.py:124
  184.0 120.5 %copy-start.30 = (f32[768]{0:T(1024)}, f32[768]{0:T(1024)S(1)}, u32[]{:S(2)}) copy-start(f32[768]{0:T(1024)S(1)} %convert_element_type.215) | copy-start | bytes 9220
  184.1 97.5 %copy-start.39 = (f32[768]{0:T(1024)}, f32[768]{0:T(1024)S(1)}, u32[]{:S(2)}) copy-start(f32[768]{0:T(1024)S(1)} %convert_element_type.216) | copy-start | bytes 9220
  213.0 91.5 %copy-start.24 = (f32[512]{0:T(512)}, f32[512]{0:T(512)S(1)}, u32[]{:S(2)}) copy-start(f32[512]{0:T(512)S(1)} %broadcast_multiply_fusion.1) | copy-start | bytes 6148
  214.5 90.1 %copy-start.33 = (f32[512]{0:T(512)}, f32[512]{0:T(512)S(1)}, u32[]{:S(2)}) copy-start(f32[512]{0:T(512)S(1)} %fusion.65) | copy-start | bytes 6148
  214.5 67.1 %copy-start.8 = (f32[512,768]{1,0:T(8,128)S(1)}, f32[512,768]{1,0:T(8,128)}, u32[]{:S(2)}) copy-start(f32[512,768]{1,0:T(8,128)} %copy-done.7) | copy-start | bytes 4718596
  281.6 6.5 copy-start.13
  289.4 2.6 copy-start.46
  291.1 9.8 slice-start
  291.9 9.0 copy-start.18
  292.0 8.9 slice-start.1
  300.9 3.6 copy-start.48
  304.6 2.6 copy-start.47
  305.2 3.9 copy-start.35
  307.2 6.2 copy-start.15
  309.1 15.9 %all-to-all-start.4 = ((bf16[512,4,192]{0,2,1:T(8,128)(2,1)}), bf16[512,4,192]{0,2,1:T(8,128)(2,1)}, u32[]{:S(2)}, u32[]{:S(2)}) async-start(bf16[512,4,192]{0,2,1:T(8,128)(2,1)} %bitcast.15), calls=%async_computation.4 | async-start | bytes 1572864 | tf_op jit(solution)/shard_map/all_to_all | solution.py:177
  313.4 244.0 %reduce-scatter.7.cloned.1.call-start = ((), (), s32[]{:S(2)}) async-start(), calls=%async_computation.17 | async-start | bytes 2654208 | tf_op jit(solution)/shard_map/reduce_scatter | solution.py:258
  316.8 14.6 %copy-start.5 = (bf16[2048,3,64]{0,2,1:T(8,128)(2,1)S(1)}, bf16[2048,3,64]{0,2,1:T(8,128)(2,1)}, u32[]{:S(2)}) copy-start(bf16[2048,3,64]{0,2,1:T(8,128)(2,1)} %copy-done.4) | copy-start | bytes 2359300
  337.7 4.5 copy-start.2
  345.7 10.8 %copy-start.3 = (f32[3,512,2048]{2,1,0:T(8,128)S(1)}, f32[3,512,2048]{2,1,0:T(8,128)}, u32[]{:S(2)}) copy-start(f32[3,512,2048]{2,1,0:T(8,128)} %copy-done.2) | copy-start | bytes 37748740 | tf_op jit(solution)/shard_map/while
  366.1 4.5 copy-start.2
  374.2 10.8 %copy-start.3 = (f32[3,512,2048]{2,1,0:T(8,128)S(1)}, f32[3,512,2048]{2,1,0:T(8,128)}, u32[]{:S(2)}) copy-start(f32[3,512,2048]{2,1,0:T(8,128)} %copy-done.2) | copy-start | bytes 37748740 | tf_op jit(solution)/shard_map/while
  395.2 4.5 copy-start.2
  403.2 10.7 %copy-start.3 = (f32[3,512,2048]{2,1,0:T(8,128)S(1)}, f32[3,512,2048]{2,1,0:T(8,128)}, u32[]{:S(2)}) copy-start(f32[3,512,2048]{2,1,0:T(8,128)} %copy-done.2) | copy-start | bytes 37748740 | tf_op jit(solution)/shard_map/while
  424.2 4.5 copy-start.2
  432.2 10.7 %copy-start.3 = (f32[3,512,2048]{2,1,0:T(8,128)S(1)}, f32[3,512,2048]{2,1,0:T(8,128)}, u32[]{:S(2)}) copy-start(f32[3,512,2048]{2,1,0:T(8,128)} %copy-done.2) | copy-start | bytes 37748740 | tf_op jit(solution)/shard_map/while
  448.6 15.1 %all-to-all-start.6 = ((bf16[4,512,192]{1,2,0:T(8,128)(2,1)}), bf16[4,512,192]{1,2,0:T(8,128)(2,1)S(1)}, u32[]{:S(2)}, u32[]{:S(2)}) async-start(bf16[4,512,192]{1,2,0:T(8,128)(2,1)} %copy.92), calls=%async_computation.6 | async-start | bytes 1572864 | tf_op jit(solution)/shard_map/all_to_all | solution.py:220
  452.1 174.0 %reduce-scatter.5.cloned.1.call-start = ((), (), s32[]{:S(2)}) async-start(), calls=%async_computation.16 | async-start | bytes 7962624 | tf_op jit(solution)/shard_map/reduce_scatter | solution.py:256
  452.1 25.6 %copy-start.14 = (bf16[4,512,3,64]{1,3,2,0:T(8,128)(2,1)S(1)}, bf16[4,512,3,64]{1,3,2,0:T(8,128)(2,1)}, u32[]{:S(2)}) copy-start(bf16[4,512,3,64]{1,3,2,0:T(8,128)(2,1)} %get-tuple-element.132) | copy-start | bytes 2359300
  463.7 14.1 %copy-start.16 = (bf16[4,512,192]{1,2,0:T(8,128)(2,1)}, bf16[4,512,192]{1,2,0:T(8,128)(2,1)S(1)}, u32[]{:S(2)}) copy-start(bf16[4,512,192]{1,2,0:T(8,128)(2,1)S(1)} %all-to-all-done.6) | copy-start | bytes 2359300
  498.4 294.3 %reduce-scatter.11.cloned.1.call-start = ((), (), s32[]{:S(2)}) async-start(), calls=%async_computation.19 | async-start | bytes 10616832 | tf_op jit(solution)/shard_map/reduce_scatter | solution.py:264
  507.8 1.4 copy-start.34
  507.8 451.4 %reduce-scatter.9.cloned.1.call-start = ((), (), s32[]{:S(2)}) async-start(), calls=%async_computation.18 | async-start | bytes 10616832 | tf_op jit(solution)/shard_map/reduce_scatter | solution.py:262
  516.4 2.7 copy-start.26
  516.4 2.7 copy-start.27
  516.4 2.7 copy-start.28
  516.4 2.7 copy-start.29
  516.4 2.7 copy-start.32
  516.4 2.7 copy-start.41
  516.4 2.7 copy-start.42
  516.5 493.4 %all-reduce.21.cloned.1.call-start = ((), (), s32[]{:S(2)}) async-start(), calls=%async_computation.20 | async-start | bytes 3538944 | tf_op jit(solution)/shard_map/psum | solution.py:285
  557.4 404.0 %copy-start.11 = (f32[512,768]{1,0:T(8,128)S(1)}, f32[512,768]{1,0:T(8,128)}, u32[]{:S(2)}) copy-start(f32[512,768]{1,0:T(8,128)} %copy-done.10) | copy-start | bytes 4718596
  557.4 404.0 %copy-start.36 = (f32[512]{0:T(512)S(1)}, f32[512]{0:T(512)}, u32[]{:S(2)}) copy-start(f32[512]{0:T(512)} %copy-done.35) | copy-start | bytes 6148
  557.4 404.0 %copy-start.44 = (pred[512]{0:T(512)(128)(4,1)S(1)}, pred[512]{0:T(512)(128)(4,1)}, u32[]{:S(2)}) copy-start(pred[512]{0:T(512)(128)(4,1)} %copy-done.43) | copy-start | bytes 1540
  961.4 5.6 copy-start.23
  961.4 6.2 copy-start.38
  967.0 49.1 %copy-start.1 = (bf16[1,10,768]{2,1,0:T(8,128)(2,1)S(1)}, bf16[1,10,768]{2,1,0:T(8,128)(2,1)}, u32[]{:S(2)}) copy-start(bf16[1,10,768]{2,1,0:T(8,128)(2,1)} %param.22) | copy-start | bytes 46084
  1009.9 4.4 copy-start.20
  1009.9 5.4 copy-start.21
  (8 other events, 9.7 us)
Sparse Core Ops, SparseCore 0:
  10.2 68.4 all-gather.5
  80.9 39.4 all-gather.7
  122.7 78.6 all-gather.9
  203.4 78.1 all-gather.11
  317.4 67.6 reduce-scatter.6
  498.5 127.5 reduce-scatter.4
  630.1 162.5 reduce-scatter.10
  796.7 162.3 reduce-scatter.8
  963.1 46.7 all-reduce.20
where the time goes:
time: 1030 us; the launch traced here: 1020 us
  waiting for transfers between devices  528 us (51%)
  matrix products  195 us (19%)
  blocking collectives  146 us (14%)
  other arithmetic  57.2 us (6%)
  local copies, waits for them, and re-layouts  50.3 us (5%)
  starting transfers between devices  22.2 us (2%)
  between operations  18.7 us (2%)
    reduce_scatter x1, waiting for transfers between devices, per_device(): lax.psum_scatter(grad_down_weight, 'fsdp', scatter_dimension=0, tiled=True)  165 us
    reduce_scatter x1, waiting for transfers between devices, per_device(): lax.psum_scatter(grad_up_weight, 'fsdp', scatter_dimension=0, tiled=True)  164 us
    unnamed x2, blocking collectives  77.3 us
    reduce_scatter x1, waiting for transfers between devices, per_device(): lax.psum_scatter(grad_qkv_weight, 'fsdp', scatter_dimension=0, tiled=True)  66.9 us
    all_gather x1, waiting for transfers between devices, per_device(): lax.all_gather(down_weight, 'fsdp', axis=0, tiled=True)  46.2 us
    all_gather x1, blocking collectives, per_device(): lax.all_gather(up_bias, 'fsdp', axis=0, tiled=True)  26.3 us
    dot_general x8, matrix products, scores_for(): jnp.einsum('qhd,khd->hqk', query_block, heads_key, preferred_element_type...  25.4 us
    dot_general x4, matrix products, over_rows(): lax.dot_general(left, right, (((0,), (0,)), ((), ())), preferred_element_...  25.2 us
  transfers between devices with their start and end apart: 15, of which 11 were waited for; matrix products, arithmetic and copies ran while one was open for 25% of the time, Pallas kernels for 0%

commit v1 on v0

--- a/solution.py
+++ b/solution.py
@@ -8,6 +8,39 @@
 MEM = 10
 norm_epsilon = 1e-06
 masked_score = -1e30
+
+
+def push_slot(my_data, along_dim):
+    my_data = jnp.moveaxis(my_data, 0, along_dim)
+    row_out = my_data.shape
+    return my_data.reshape(
+        *row_out[:along_dim], row_out[along_dim] * row_out[along_dim + 1], *row_out[along_dim + 2 :]
+    )
+
+
+def _drive_lane(vector, chip_axis, axis_k):
+    n_shards = lax.axis_size(chip_axis)
+    buffer = []
+    for at in range(n_shards):
+        buffer.append((at, (at + 1) % n_shards))
+    rack = []
+    for ii, h in buffer:
+        rack.append((h, ii))
+    later, seen_now = ([], [])
+    for q in range(n_shards - 1):
+        if q % 2 == 0:
+            later.append(
+                lax.ppermute(later[-1] if later else vector, axis_name=chip_axis, perm=buffer)
+            )
+        else:
+            seen_now.append(
+                lax.ppermute(seen_now[-1] if seen_now else vector, axis_name=chip_axis, perm=rack)
+            )
+    p_next = jnp.stack([*later[::-1], vector, *seen_now])
+    y2 = lax.axis_index(chip_axis)
+    placed = y2 - len(later)
+    p_next = p_next[(jnp.arange(n_shards) - placed) % n_shards]
+    return push_slot(p_next, axis_k)
 
 
 def normalize(values, gain_vec, shift_vec):
@@ -132,7 +165,7 @@
     up_full, up_bias_full, down_full, down_bias_full, gain_two, shift_two = (
         lax.all_gather(up_weight, "fsdp", axis=0, tiled=True),
         lax.all_gather(up_bias, "fsdp", axis=0, tiled=True),
-        lax.all_gather(down_weight, "fsdp", axis=0, tiled=True),
+        _drive_lane(down_weight, "fsdp", 0),
         lax.all_gather(down_bias, "fsdp", axis=0, tiled=True),
         lax.all_gather(norm2_gain, "fsdp", axis=0, tiled=True),
         lax.all_gather(norm2_bias, "fsdp", axis=0, tiled=True),

time: 1030 us -> 1070 us (1.039)
  blocking collectives: 146 us -> 176 us
  waiting for transfers between devices: 528 us -> 503 us
  local copies, waits for them, and re-layouts: 50.3 us -> 69 us
  starting transfers between devices: 22.2 us -> 37.4 us
    ppermute x0 -> x7, waiting for transfers between devices: none -> 22.7 us  [the longest x4 22.7 us: _drive_lane(): lax.ppermute(later[-1] if later else vector, axis_name=chip_axis, perm=bu...]
    all_gather x1, blocking collectives: 26.3 us -> 46.4 us  [per_device(): lax.all_gather(up_bias, 'fsdp', axis=0, tiled=True)]
    all_gather x1, waiting for transfers between devices: 18.2 us -> 0.01 us  [per_device(): lax.all_gather(qkv_weight, 'fsdp', axis=0, tiled=True)]
    ppermute x0 -> x7, starting transfers between devices: none -> 14.6 us  [the longest x3 11.6 us: _drive_lane(): lax.ppermute(seen_now[-1] if seen_now else vector, axis_name=chip_axis, p...]
    unnamed x124 -> x143, local copies, waits for them, and re-layouts: 16.2 us -> 27.3 us
  transfers between devices with their start and end apart: 15 -> 22, of which waited for: 11 -> 11; matrix products, arithmetic and copies ran while one was open for 25% -> 27% of each run, Pallas kernels for 0% -> 0%
where the time goes in v1:
time: 1070 us
  waiting for transfers between devices  503 us (47%)
  matrix products  195 us (18%)
  blocking collectives  176 us (16%)
  local copies, waits for them, and re-layouts  69 us (6%)
  other arithmetic  60.4 us (6%)
  starting transfers between devices  37.4 us (3%)
  between operations  18.9 us (2%)
    reduce_scatter x1, waiting for transfers between devices, per_device(): lax.psum_scatter(grad_down_weight, 'fsdp', scatter_dimension=0, tiled=True)  164 us
    reduce_scatter x1, waiting for transfers between devices, per_device(): lax.psum_scatter(grad_up_weight, 'fsdp', scatter_dimension=0, tiled=True)  164 us
    unnamed x2, blocking collectives  87.4 us
    reduce_scatter x1, waiting for transfers between devices, per_device(): lax.psum_scatter(grad_qkv_weight, 'fsdp', scatter_dimension=0, tiled=True)  67.1 us
    all_gather x1, blocking collectives, per_device(): lax.all_gather(up_bias, 'fsdp', axis=0, tiled=True)  46.4 us
    all_gather x1, waiting for transfers between devices, per_device(): lax.all_gather(down_weight, 'fsdp', axis=0, tiled=True)  38.8 us
    unnamed x143, local copies, waits for them, and re-layouts  27.3 us
    dot_general x4, matrix products, over_rows(): lax.dot_general(left, right, (((0,), (0,)), ((), ())), preferred_element_...  25.4 us
  transfers between devices with their start and end apart: 22, of which 11 were waited for; matrix products, arithmetic and copies ran while one was open for 27% of the time, Pallas kernels for 0%

profile of v1, /device:TPU:0, one launch (start us, length us, event | category | flops | bytes accessed | tf_op | source)
XLA Modules:
  0.0 1065.2 jit_solution(6285369589855746505)
XLA Ops:
  9.4 3.0 collective-permute-start
  12.4 3.1 collective-permute-start.4
  24.7 49.9 %all-reduce.16 = (bf16[1536]{0:T(1024)(128)(2,1)S(1)}, bf16[768]{0:T(1024)(128)(2,1)S(1)}, bf16[768]{0:T(1024)(128)(2,1)S(1)}, bf16[768]{0:T(1024)(128)(2,1)S(1)...) all-reduce(bf16[1536]{0:T(1024)(128)(2,1)S(1)} %dynamic-update-slic, ...), channel_id=1, replica_groups=mesh['fsdp'=8,'seq'=4] {'fsdp'}, use_global_device_ids=true, to_apply=%add | all-reduce | flops 6144 | bytes 24576
  76.8 22.7 %collective-permute-done.1 = bf16[384,768]{1,0:T(8,128)(2,1)S(1)} collective-permute-done((bf16[384,768]{1,0:T(8,128)(2,1)S(1)}, bf16[384,768]{1,0:T(8,128)(2,1)S(1)}, u32[]{:S(2)}, u32[]{:S(2)}) %collective-permute-start.1) | collective-permute-done | bytes 589856 | tf_op jit(solution)/shard_map/ppermute | solution.py:33
  99.5 4.2 fusion.82
  107.4 3.5 all-to-all-start
  111.0 4.6 collective-permute-start.5
  115.7 46.4 %all-gather = bf16[8,1,384]{2,1,0:T(2,128)(2,1)S(1)} all-gather(bf16[1,1,384]{2,1,0:T(2,128)(2,1)S(1)} %reshape.265), channel_id=1, replica_groups=mesh['fsdp'=8,'seq'=4] {'fsdp'}, dimensions={0}, use_global_device_ids=true | all-gather | bytes 6912 | tf_op jit(solution)/shard_map/all_gather | solution.py:167
  165.1 3.5 all-to-all-start.2
  169.1 3.9 collective-permute-start.6
  180.2 3.7 all-to-all-start.1
  200.0 44.2 %while.30 = (s32[]{:T(128)}, bf16[4,512,3,64]{1,3,2,0:T(8,128)(2,1)}, f32[4,3,512,1]{2,1,3,0:T(4,128)S(1)}, f32[4,3,512,1]{2,1,3,0:T(4,128)S(1)}, s32[4]{0:T(128...) while((s32[]{:T(128)}, ...), condition=%wide.region_4.5_spmd.clone, body=%wide.region_1.4_spmd.clone.sunk | while | flops 843152384 | bytes 39787204 | solution.py:153
  206.7 4.3 fusion.135
  217.8 4.3 fusion.135
  228.8 4.3 fusion.135
  239.9 4.3 fusion.135
  244.2 3.9 all-to-all-start.3
  254.0 5.6 gather_fusion
  262.8 19.6 %multiply_convert_fusion.1 = (bf16[512,3072]{1,0:T(8,128)(2,1)S(1)}, f32[512,3072]{1,0:T(8,128)}, f32[512,3072]{1,0:T(8,128)}) fusion(f32[3072]{0:T(1024)S(1)} %bitcast.174, bf16[768,3072]{1,0:T(8,128)(2,1)} %all-gather.10.cloned.1.call-done, f32[512,768]{1,0:T(8,128)S(1)} %get-tuple-element.399, f32[768]{0:T(1024)S(1)} %convert_element_type.216, ...), kind=kOutput, calls=%fused_computation.50 | convolution fusion | flops 2521694208 | bytes 22042624 | tf_op jit(solution)/shard_map/dot_general | solution.py:174
  289.6 38.8 %all-gather.12.cloned.1.call-done = bf16[3072,768]{1,0:T(8,128)(2,1)} async-done(((bf16[384,768]{1,0:T(8,128)(2,1)}), bf16[3072,768]{1,0:T(8,128)(2,1)}) %all-gather.12.cloned.1.call-update) | async-done | bytes 4718608 | tf_op jit(solution)/shard_map/all_gather | solution.py:188
  328.4 9.5 convert_reduce_fusion
  337.9 7.2 multiply_reduce_fusion.2
  350.5 4.2 all-to-all-start.4
  354.8 3.6 fusion.83
  358.4 8.0 all-to-all-done.4
  372.8 115.5 %while.31 = (s32[]{:T(128)}, f32[2048,3,64]{0,2,1:T(8,128)S(1)}, f32[2048,3,64]{0,2,1:T(8,128)}, bf16[4,512,3,64]{1,3,2,0:T(8,128)(2,1)}, s32[4]{0:T(128)S(1)}, ...) while((s32[]{:T(128)}, f32[2048,3,64]{0,2,1:T(8,128)S(1)}, ...), condition=%wide.region_15.16_spmd.clone, body=%wide.region_13.15_spmd.clone.sunk | while | flops 2046886400 | bytes 204722992 | solution.py:243
  374.7 4.3 exponential_divide_fusion.2
  379.1 3.2 multiply_reduce_fusion.8
  383.6 3.5 multiply_convert_fusion.3
  387.1 4.5 fusion.145
  391.6 6.3 fusion.147
  397.9 3.4 fusion.146
  403.2 4.3 exponential_divide_fusion.2
  407.6 3.2 multiply_reduce_fusion.8
  412.1 3.5 multiply_convert_fusion.3
  415.6 4.5 fusion.145
  420.1 6.3 fusion.147
  426.4 4.0 fusion.146
  432.3 4.3 exponential_divide_fusion.2
  436.7 3.2 multiply_reduce_fusion.8
  441.2 3.5 multiply_convert_fusion.3
  444.7 4.4 fusion.145
  449.1 6.3 fusion.147
  455.4 4.0 fusion.146
  461.3 4.3 exponential_divide_fusion.2
  465.7 3.2 multiply_reduce_fusion.8
  470.2 3.5 multiply_convert_fusion.3
  473.7 4.4 fusion.145
  478.1 6.3 fusion.147
  484.4 4.0 fusion.146
  490.1 3.6 all-to-all-start.6
  496.0 9.3 all-to-all-done.6
  505.3 14.1 %all_to_all.134 = bf16[4,512,192]{1,2,0:T(8,128)(2,1)S(1)} all-to-all(bf16[4,512,192]{1,2,0:T(8,128)(2,1)S(1)} %copy.93), channel_id=1, replica_groups=mesh['fsdp'=8,'seq'=4] {'seq'}, dimensions={0} | all-to-all | bytes 1572864 | tf_op jit(solution)/shard_map/all_to_all | solution.py:254
  519.4 14.3 %all_to_all.135 = bf16[4,512,192]{1,2,0:T(8,128)(2,1)S(1)} all-to-all(bf16[4,512,192]{1,2,0:T(8,128)(2,1)S(1)} %bitcast.169), channel_id=1, replica_groups=mesh['fsdp'=8,'seq'=4] {'seq'}, dimensions={0} | all-to-all | bytes 1572864 | tf_op jit(solution)/shard_map/all_to_all | solution.py:252
  533.6 6.4 fusion.51
  541.2 8.2 fusion.84
  550.8 7.2 fusion.71
  560.9 37.5 %all-reduce.15 = (bf16[1536]{0:T(1024)(128)(2,1)S(1)}, bf16[768]{0:T(1024)(128)(2,1)S(1)}, bf16[768]{0:T(1024)(128)(2,1)S(1)}, bf16[768]{0:T(1024)(128)(2,1)S(1)...) all-reduce(f32[1536]{0:T(1024)S(1)} %pad_maximum_fusion.3, ...), channel_id=3, replica_groups=mesh['fsdp'=8,'seq'=4] {'fsdp'}, use_global_device_ids=true, to_apply=%region_22.23.clone | all-reduce | flops 9216 | bytes 55296
  600.7 67.1 %reduce-scatter.5.cloned.1.call-done = f32[96,2304]{1,0:T(8,128)} async-done(((f32[768,2304]{1,0:T(8,128)}), f32[96,2304]{1,0:T(8,128)}) %reduce-scatter.5.cloned.1.call-update) | async-done | bytes 884752 | tf_op jit(solution)/shard_map/reduce_scatter | solution.py:289
  669.7 164.4 %reduce-scatter.11.cloned.1.call-done = f32[384,768]{1,0:T(8,128)} async-done(((f32[3072,768]{1,0:T(8,128)}), f32[384,768]{1,0:T(8,128)}) %reduce-scatter.11.cloned.1.call-update) | async-done | bytes 1179664 | tf_op jit(solution)/shard_map/reduce_scatter | solution.py:297
  836.3 164.3 %reduce-scatter.9.cloned.1.call-done = f32[96,3072]{1,0:T(8,128)} async-done(((f32[768,3072]{1,0:T(8,128)}), f32[96,3072]{1,0:T(8,128)}) %reduce-scatter.9.cloned.1.call-update) | async-done | bytes 1179664 | tf_op jit(solution)/shard_map/reduce_scatter | solution.py:295
  1002.9 5.6 broadcast_select_fusion
  1009.7 14.3 %all-reduce.17 = (bf16[1,10,768]{2,1,0:T(8,128)(2,1)S(1)}, bf16[1,10,768]{2,1,0:T(8,128)(2,1)S(1)}, bf16[192]{0:T(256)(128)(2,1)S(1)}, bf16[96]{0:T(256)(128)(2,...) all-reduce(bf16[1,10,768]{2,1,0:T(8,128)(2,1)S(1)} %fusion.49, ...), channel_id=1, replica_groups=mesh['fsdp'=8,'seq'=4] {'seq'}, use_global_device_ids=true, to_apply=%region_16.17 | all-reduce | flops 16512 | bytes 66048 | tf_op jit(solution)/shard_map/psum | solution.py:330
  1029.4 21.9 %all-reduce.21.cloned.1.call-done = (bf16[96,2304]{1,0:T(8,128)(2,1)}, bf16[96,768]{1,0:T(8,128)(2,1)}, bf16[96,3072]{1,0:T(8,128)(2,1)}, bf16[384,768]{1,0:T(8,128)(2,1)}) async-done(((bf16[96,2304]{1,0:T(8,128)(2,1)}, bf16[96,768]{1,0:T(8,128)(2,1)}, bf16[96,3072]{1,0:T(8,128)(2,1)}, bf16[384,768]{1,0:T(8,128)(2,1)}), (bf16[96,2304]{1,0:T(8,128)(2,1)}, bf16[96,768]{1,0:T(8,128)(2,1)}, ...) | async-done | bytes 1769488 | tf_op jit(solution)/shard_map/psum | solution.py:318
  (312 shorter events, 133.9 us)
Async XLA Ops:
  7.2 67.6 %copy-start = (bf16[1,10,768]{2,1,0:T(8,128)(2,1)S(1)}, bf16[1,10,768]{2,1,0:T(8,128)(2,1)}, u32[]{:S(2)}) copy-start(bf16[1,10,768]{2,1,0:T(8,128)(2,1)} %param.22) | copy-start | bytes 46084
  7.2 92.3 %all-gather.6.cloned.1.call-start = ((), (), s32[]{:S(2)}) async-start(), calls=%async_computation.12 | async-start | bytes 3981312 | tf_op jit(solution)/shard_map/all_gather | solution.py:112
  7.9 251.6 %all-gather.8.cloned.1.call-start = ((), (), s32[]{:S(2)}) async-start(), calls=%async_computation.13 | async-start | bytes 1327104 | tf_op jit(solution)/shard_map/all_gather | solution.py:114
  8.7 254.1 %all-gather.10.cloned.1.call-start = ((), (), s32[]{:S(2)}) async-start(), calls=%async_computation.14 | async-start | bytes 5308416 | tf_op jit(solution)/shard_map/all_gather | solution.py:166
  9.4 65.1 %collective-permute-start = (bf16[384,768]{1,0:T(8,128)(2,1)}, bf16[384,768]{1,0:T(8,128)(2,1)S(1)}, u32[]{:S(2)}, u32[]{:S(2)}) collective-permute-start(bf16[384,768]{1,0:T(8,128)(2,1)} %param.33), channel_id=1, source_target_pairs={{0,4},{4,8},{8,12},{12,16},{16,20},{20,24},{24,28},{28,0},{1,5},{5... | collective-permute-start | bytes 1769480 | tf_op jit(solution)/shard_map/ppermute | solution.py:33
  12.4 98.5 %collective-permute-start.4 = (bf16[384,768]{1,0:T(8,128)(2,1)}, bf16[384,768]{1,0:T(8,128)(2,1)S(1)}, u32[]{:S(2)}, u32[]{:S(2)}) collective-permute-start(bf16[384,768]{1,0:T(8,128)(2,1)} %param.33), channel_id=1, source_target_pairs={{4,0},{8,4},{12,8},{16,12},{20,16},{24,20},{28,24},{0,28},{5,1},{9... | collective-permute-start | bytes 1769480 | tf_op jit(solution)/shard_map/ppermute | solution.py:37
  74.5 29.2 %copy-start.43 = (s32[10]{0:T(128)}, s32[10]{0:T(128)S(1)}, u32[]{:S(2)}) copy-start(s32[10]{0:T(128)S(1)} %iota_add_fusion.1) | copy-start | bytes 124
  74.5 29.2 %copy-start.26 = (s32[512]{0:T(512)}, s32[512]{0:T(512)S(1)}, u32[]{:S(2)}) copy-start(s32[512]{0:T(512)S(1)} %iota_add_fusion) | copy-start | bytes 6148
  74.6 29.2 %copy-start.23 = (bf16[384,768]{1,0:T(8,128)(2,1)}, bf16[384,768]{1,0:T(8,128)(2,1)S(1)}, u32[]{:S(2)}) copy-start(bf16[384,768]{1,0:T(8,128)(2,1)S(1)} %collective-permute-done) | copy-start | bytes 1769476
  74.6 25.0 %collective-permute-start.1 = (bf16[384,768]{1,0:T(8,128)(2,1)S(1)}, bf16[384,768]{1,0:T(8,128)(2,1)S(1)}, u32[]{:S(2)}, u32[]{:S(2)}) collective-permute-start(bf16[384,768]{1,0:T(8,128)(2,1)S(1)} %collective-permute-done), channel_id=1, source_target_pairs={{0,4},{4,8},{8,12},{12,16},{16,20},{20,24},{24,28},{28,0},{1,5},{5... | collective-permute-start | bytes 1769480 | tf_op jit(solution)/shard_map/ppermute | solution.py:33
  74.7 29.1 %copy-start.51 = (pred[512]{0:T(512)(128)(4,1)}, pred[512]{0:T(512)(128)(4,1)S(1)}, u32[]{:S(2)}) copy-start(pred[512]{0:T(512)(128)(4,1)S(1)} %fusion.54) | copy-start | bytes 1540
  76.8 27.0 %copy-start.19 = (bf16[512,768]{1,0:T(8,128)(2,1)}, bf16[512,768]{1,0:T(8,128)(2,1)S(1)}, u32[]{:S(2)}) copy-start(bf16[512,768]{1,0:T(8,128)(2,1)S(1)} %fusion.47) | copy-start | bytes 2359300
  99.5 4.3 copy-start.24
  99.5 16.0 %collective-permute-start.2 = (bf16[384,768]{1,0:T(8,128)(2,1)S(1)}, bf16[384,768]{1,0:T(8,128)(2,1)S(1)}, u32[]{:S(2)}, u32[]{:S(2)}) collective-permute-start(bf16[384,768]{1,0:T(8,128)(2,1)S(1)} %collective-permute-done.1), channel_id=1, source_target_pairs={{0,4},{4,8},{8,12},{12,16},{16,20},{20,24},{24,28},{28,0},{1,5},{5... | collective-permute-start | bytes 1769480 | tf_op jit(solution)/shard_map/ppermute | solution.py:33
  103.8 11.8 %copy-start.53 = (bf16[384]{0:T(512)(128)(2,1)S(1)}, bf16[384]{0:T(512)(128)(2,1)}, u32[]{:S(2)}) copy-start(bf16[384]{0:T(512)(128)(2,1)} %param.32) | copy-start | bytes 2308
  107.4 57.7 %all-to-all-start = ((bf16[512,4,192]{0,2,1:T(8,128)(2,1)}), bf16[512,4,192]{0,2,1:T(8,128)(2,1)S(1)}, u32[]{:S(2)}, u32[]{:S(2)}) async-start(bf16[512,4,192]{0,2,1:T(8,128)(2,1)} %bitcast.4), calls=%async_computation | async-start | bytes 1572864 | tf_op jit(solution)/shard_map/all_to_all | solution.py:125
  110.9 217.5 %all-gather.12.cloned.1.call-start = ((), (), s32[]{:S(2)}) async-start(), calls=%async_computation.15 | async-start | bytes 5308416 | tf_op jit(solution)/shard_map/all_gather | solution.py:188
  111.0 62.9 %copy-start.22 = (bf16[384,768]{1,0:T(8,128)(2,1)}, bf16[384,768]{1,0:T(8,128)(2,1)S(1)}, u32[]{:S(2)}) copy-start(bf16[384,768]{1,0:T(8,128)(2,1)S(1)} %collective-permute-done.4) | copy-start | bytes 1769476
  111.0 58.1 %collective-permute-start.5 = (bf16[384,768]{1,0:T(8,128)(2,1)S(1)}, bf16[384,768]{1,0:T(8,128)(2,1)}, u32[]{:S(2)}, u32[]{:S(2)}) collective-permute-start(bf16[384,768]{1,0:T(8,128)(2,1)S(1)} %collective-permute-done.4), channel_id=1, source_target_pairs={{4,0},{8,4},{12,8},{16,12},{20,16},{24,20},{28,24},{0,28},{5,1},{9... | collective-permute-start | bytes 1769480 | tf_op jit(solution)/shard_map/ppermute | solution.py:37
  115.5 57.5 %collective-permute-start.3 = (bf16[384,768]{1,0:T(8,128)(2,1)S(1)}, bf16[384,768]{1,0:T(8,128)(2,1)S(1)}, u32[]{:S(2)}, u32[]{:S(2)}) collective-permute-start(bf16[384,768]{1,0:T(8,128)(2,1)S(1)} %collective-permute-done.2), channel_id=1, source_target_pairs={{0,4},{4,8},{8,12},{12,16},{16,20},{20,24},{24,28},{28,0},{1,5},{5... | collective-permute-start | bytes 1769480 | tf_op jit(solution)/shard_map/ppermute | solution.py:33
  115.6 229.5 %copy-start.36 = (f32[768]{0:T(1024)}, f32[768]{0:T(1024)S(1)}, u32[]{:S(2)}) copy-start(f32[768]{0:T(1024)S(1)} %convert_element_type.215) | copy-start | bytes 9220
  115.6 166.9 %copy-start.45 = (f32[768]{0:T(1024)}, f32[768]{0:T(1024)S(1)}, u32[]{:S(2)}) copy-start(f32[768]{0:T(1024)S(1)} %convert_element_type.216) | copy-start | bytes 9220
  165.1 15.1 %all-to-all-start.2 = ((bf16[512,4,192]{0,2,1:T(8,128)(2,1)}), bf16[512,4,192]{0,2,1:T(8,128)(2,1)S(1)}, u32[]{:S(2)}, u32[]{:S(2)}) async-start(bf16[512,4,192]{0,2,1:T(8,128)(2,1)} %bitcast.8), calls=%async_computation.2 | async-start | bytes 1572864 | tf_op jit(solution)/shard_map/all_to_all | solution.py:127
  169.1 83.0 %collective-permute-start.6 = (bf16[384,768]{1,0:T(8,128)(2,1)}, bf16[384,768]{1,0:T(8,128)(2,1)}, u32[]{:S(2)}, u32[]{:S(2)}) collective-permute-start(bf16[384,768]{1,0:T(8,128)(2,1)} %collective-permute-done.5), channel_id=1, source_target_pairs={{4,0},{8,4},{12,8},{16,12},{20,16},{24,20},{28,24},{0,28},{5,1},{9... | collective-permute-start | bytes 1769480 | tf_op jit(solution)/shard_map/ppermute | solution.py:37
  180.2 15.3 %all-to-all-start.1 = ((bf16[512,4,192]{0,2,1:T(8,128)(2,1)}), bf16[512,4,192]{0,2,1:T(8,128)(2,1)S(1)}, u32[]{:S(2)}, u32[]{:S(2)}) async-start(bf16[512,4,192]{0,2,1:T(8,128)(2,1)} %bitcast.6), calls=%async_computation.1 | async-start | bytes 1572864 | tf_op jit(solution)/shard_map/all_to_all | solution.py:126
  244.2 15.4 %copy-start.4 = (bf16[2048,3,64]{0,2,1:T(8,128)(2,1)}, bf16[2048,3,64]{0,2,1:T(8,128)(2,1)S(1)}, u32[]{:S(2)}) copy-start(bf16[2048,3,64]{0,2,1:T(8,128)(2,1)S(1)} %get-tuple-element.654) | copy-start | bytes 2359300
  244.2 15.4 %copy-start.6 = (bf16[2048,3,64]{0,2,1:T(8,128)(2,1)}, bf16[2048,3,64]{0,2,1:T(8,128)(2,1)S(1)}, u32[]{:S(2)}) copy-start(bf16[2048,3,64]{0,2,1:T(8,128)(2,1)S(1)} %get-tuple-element.655) | copy-start | bytes 2359300
  244.2 15.5 %all-to-all-start.3 = ((bf16[4,512,192]{1,2,0:T(8,128)(2,1)}), bf16[4,512,192]{1,2,0:T(8,128)(2,1)S(1)}, u32[]{:S(2)}, u32[]{:S(2)}) async-start(bf16[4,512,192]{1,2,0:T(8,128)(2,1)} %bitcast.10), calls=%async_computation.3 | async-start | bytes 1572864 | tf_op jit(solution)/shard_map/all_to_all | solution.py:157
  259.7 22.8 %copy-start.16 = (bf16[4,512,192]{1,2,0:T(8,128)(2,1)}, bf16[4,512,192]{1,2,0:T(8,128)(2,1)S(1)}, u32[]{:S(2)}) copy-start(bf16[4,512,192]{1,2,0:T(8,128)(2,1)S(1)} %all-to-all-done.3) | copy-start | bytes 2359300
  262.4 20.1 %copy-start.7 = (f32[512,768]{1,0:T(8,128)}, f32[512,768]{1,0:T(8,128)S(1)}, u32[]{:S(2)}) copy-start(f32[512,768]{1,0:T(8,128)S(1)} %get-tuple-element.399) | copy-start | bytes 4718596
  262.4 82.7 %copy-start.29 = (f32[512]{0:T(512)}, f32[512]{0:T(512)S(1)}, u32[]{:S(2)}) copy-start(f32[512]{0:T(512)S(1)} %broadcast_multiply_fusion.1) | copy-start | bytes 6148
  262.8 82.3 %copy-start.39 = (f32[512]{0:T(512)}, f32[512]{0:T(512)S(1)}, u32[]{:S(2)}) copy-start(f32[512]{0:T(512)S(1)} %fusion.65) | copy-start | bytes 6148
  262.8 19.7 %copy-start.12 = (bf16[8,384,768]{2,1,0:T(8,128)(2,1)S(1)}, bf16[8,384,768]{2,1,0:T(8,128)(2,1)}, u32[]{:S(2)}) copy-start(bf16[8,384,768]{2,1,0:T(8,128)(2,1)} %gather_fusion) | copy-start | bytes 14155780
  262.8 19.7 %copy-start.47 = (f32[768]{0:T(1024)S(1)}, f32[768]{0:T(1024)}, u32[]{:S(2)}) copy-start(f32[768]{0:T(1024)} %convert_element_type.220) | copy-start | bytes 9220
  282.6 4.5 copy-start.31
  289.6 48.3 %copy-start.20 = (bf16[512,768]{1,0:T(8,128)(2,1)}, bf16[512,768]{1,0:T(8,128)(2,1)S(1)}, u32[]{:S(2)}) copy-start(bf16[512,768]{1,0:T(8,128)(2,1)S(1)} %get-tuple-element.372) | copy-start | bytes 2359300
  328.4 9.5 copy-start.8
  337.9 7.2 copy-start.56
  345.7 12.7 %copy-start.41 = (f32[512]{0:T(512)}, f32[512]{0:T(512)S(1)}, u32[]{:S(2)}) copy-start(f32[512]{0:T(512)S(1)} %negate_multiply_fusion.1) | copy-start | bytes 6148
  350.5 15.9 %all-to-all-start.4 = ((bf16[512,4,192]{0,2,1:T(8,128)(2,1)}), bf16[512,4,192]{0,2,1:T(8,128)(2,1)}, u32[]{:S(2)}, u32[]{:S(2)}) async-start(bf16[512,4,192]{0,2,1:T(8,128)(2,1)} %bitcast.25), calls=%async_computation.4 | async-start | bytes 1572864 | tf_op jit(solution)/shard_map/all_to_all | solution.py:210
  354.7 244.3 %reduce-scatter.7.cloned.1.call-start = ((), (), s32[]{:S(2)}) async-start(), calls=%async_computation.17 | async-start | bytes 2654208 | tf_op jit(solution)/shard_map/reduce_scatter | solution.py:291
  354.8 18.0 %copy-start.5 = (bf16[2048,3,64]{0,2,1:T(8,128)(2,1)S(1)}, bf16[2048,3,64]{0,2,1:T(8,128)(2,1)}, u32[]{:S(2)}) copy-start(bf16[2048,3,64]{0,2,1:T(8,128)(2,1)} %copy-done.4) | copy-start | bytes 2359300
  379.1 4.5 copy-start.2
  387.1 10.8 %copy-start.3 = (f32[3,512,2048]{2,1,0:T(8,128)S(1)}, f32[3,512,2048]{2,1,0:T(8,128)}, u32[]{:S(2)}) copy-start(f32[3,512,2048]{2,1,0:T(8,128)} %copy-done.2) | copy-start | bytes 37748740 | tf_op jit(solution)/shard_map/while
  407.6 4.5 copy-start.2
  415.6 10.8 %copy-start.3 = (f32[3,512,2048]{2,1,0:T(8,128)S(1)}, f32[3,512,2048]{2,1,0:T(8,128)}, u32[]{:S(2)}) copy-start(f32[3,512,2048]{2,1,0:T(8,128)} %copy-done.2) | copy-start | bytes 37748740 | tf_op jit(solution)/shard_map/while
  436.7 4.5 copy-start.2
  444.7 10.7 %copy-start.3 = (f32[3,512,2048]{2,1,0:T(8,128)S(1)}, f32[3,512,2048]{2,1,0:T(8,128)}, u32[]{:S(2)}) copy-start(f32[3,512,2048]{2,1,0:T(8,128)} %copy-done.2) | copy-start | bytes 37748740 | tf_op jit(solution)/shard_map/while
  465.6 4.5 copy-start.2
  473.7 10.7 %copy-start.3 = (f32[3,512,2048]{2,1,0:T(8,128)S(1)}, f32[3,512,2048]{2,1,0:T(8,128)}, u32[]{:S(2)}) copy-start(f32[3,512,2048]{2,1,0:T(8,128)} %copy-done.2) | copy-start | bytes 37748740 | tf_op jit(solution)/shard_map/while
  490.1 29.3 %copy-start.15 = (bf16[4,512,3,64]{1,3,2,0:T(8,128)(2,1)S(1)}, bf16[4,512,3,64]{1,3,2,0:T(8,128)(2,1)}, u32[]{:S(2)}) copy-start(bf16[4,512,3,64]{1,3,2,0:T(8,128)(2,1)} %get-tuple-element.132) | copy-start | bytes 2359300
  490.1 15.3 %all-to-all-start.6 = ((bf16[4,512,192]{1,2,0:T(8,128)(2,1)}), bf16[4,512,192]{1,2,0:T(8,128)(2,1)S(1)}, u32[]{:S(2)}, u32[]{:S(2)}) async-start(bf16[4,512,192]{1,2,0:T(8,128)(2,1)} %copy.92), calls=%async_computation.6 | async-start | bytes 1572864 | tf_op jit(solution)/shard_map/all_to_all | solution.py:253
  493.7 174.0 %reduce-scatter.5.cloned.1.call-start = ((), (), s32[]{:S(2)}) async-start(), calls=%async_computation.16 | async-start | bytes 7962624 | tf_op jit(solution)/shard_map/reduce_scatter | solution.py:289
  505.3 14.1 %copy-start.18 = (bf16[4,512,192]{1,2,0:T(8,128)(2,1)}, bf16[4,512,192]{1,2,0:T(8,128)(2,1)S(1)}, u32[]{:S(2)}) copy-start(bf16[4,512,192]{1,2,0:T(8,128)(2,1)S(1)} %all-to-all-done.6) | copy-start | bytes 2359300
  540.1 294.1 %reduce-scatter.11.cloned.1.call-start = ((), (), s32[]{:S(2)}) async-start(), calls=%async_computation.19 | async-start | bytes 10616832 | tf_op jit(solution)/shard_map/reduce_scatter | solution.py:297
  549.4 451.2 %reduce-scatter.9.cloned.1.call-start = ((), (), s32[]{:S(2)}) async-start(), calls=%async_computation.18 | async-start | bytes 10616832 | tf_op jit(solution)/shard_map/reduce_scatter | solution.py:295
  558.1 444.7 %copy-start.11 = (f32[512,768]{1,0:T(8,128)S(1)}, f32[512,768]{1,0:T(8,128)}, u32[]{:S(2)}) copy-start(f32[512,768]{1,0:T(8,128)} %copy-done.10) | copy-start | bytes 4718596
  558.1 444.7 %copy-start.42 = (f32[512]{0:T(512)S(1)}, f32[512]{0:T(512)}, u32[]{:S(2)}) copy-start(f32[512]{0:T(512)} %copy-done.41) | copy-start | bytes 6148
  558.1 444.7 %copy-start.52 = (pred[512]{0:T(512)(128)(4,1)S(1)}, pred[512]{0:T(512)(128)(4,1)}, u32[]{:S(2)}) copy-start(pred[512]{0:T(512)(128)(4,1)} %copy-done.51) | copy-start | bytes 1540
  558.1 493.3 %all-reduce.21.cloned.1.call-start = ((), (), s32[]{:S(2)}) async-start(), calls=%async_computation.20 | async-start | bytes 3538944 | tf_op jit(solution)/shard_map/psum | solution.py:318
  1002.8 5.6 copy-start.27
  1002.8 6.2 copy-start.44
  1002.9 55.6 %copy-start.1 = (bf16[1,10,768]{2,1,0:T(8,128)(2,1)S(1)}, bf16[1,10,768]{2,1,0:T(8,128)(2,1)}, u32[]{:S(2)}) copy-start(bf16[1,10,768]{2,1,0:T(8,128)(2,1)} %param.22) | copy-start | bytes 46084
  1051.4 6.4 copy-start.25
  (21 other events, 48.1 us)
Sparse Core Ops, SparseCore 0:
  10.2 81.7 all-gather.5
  94.2 59.5 all-gather.7
  156.0 92.1 all-gather.9
  250.2 78.1 all-gather.11
  358.8 67.5 reduce-scatter.6
  540.2 127.5 reduce-scatter.4
  671.8 162.3 reduce-scatter.10
  838.2 162.3 reduce-scatter.8
  1004.6 46.7 all-reduce.20
